TPU v7x, 32 devices: a whole 2x2x4 slice. The times are simulated.
32 devices in a mesh: snap: 4 (over y, x), height: 8 (over z, core).
Axes of the slice: x: 2, y: 2, z: 4, core: 2. Of those that a mesh axis runs over, the one named last changes fastest.
Arguments:
- resolved: bfloat16 [64, 3, 128, 16, 2, 128], P('snap', None, 'height'), may hold values from -6 to 6
- drain: bfloat16 [64, 3, 128, 16, 2, 128], P('snap', None, 'height'), may hold values from -6 to 6
- pair_list: int32 [64, 2], replicated, may hold values from 0 to 127, as said below
- ridge_index: int32 [64], replicated, may hold values from 0 to 3
Outputs:
- predicted: float32 [64, 3, 128, 2, 64], P('snap', None, 'height')
- misfit: float32 [1], replicated
Inputs may be any that keep to these rules, and one draw needn't show every extreme that they name: `pair_list`: each row names a streamwise mode below 16 and a spanwise wavenumber below 128; no row repeats.
All inputs are finite; a program needn't handle non-finite values.
Results may differ from a plain program's by a relative error of at most 0.0032.
Values sent between devices are 32-bit elements; how exact they have to be, the bound alone decides.
A program may use at most 128 MiB of HBM per device.

v0:
```python
import functools
import math

import jax
import jax.numpy as jnp
from jax import lax
from jax.experimental import pallas as pl
from jax.experimental.pallas import tpu as pltpu
from jax.sharding import PartitionSpec as P

HIGHEST = lax.Precision.HIGHEST
CHUNK = 8
LANES = 128


def pair_tables(pair_list, points, mode_count):
    grid = jnp.arange(points, dtype=jnp.int32)
    ordered = jnp.repeat(pair_list, 2, axis=0)
    imaginary = (jnp.arange(ordered.shape[0], dtype=jnp.int32) % 2 == 1)[None, :]
    phase = grid[:, None] * ordered[None, :, 1] % points
    theta = phase.astype(jnp.float32) * (2.0 * math.pi / points)
    scaling = 1.0 / math.sqrt(points)
    cosine = jnp.cos(theta) * scaling
    sine = jnp.sin(theta) * scaling
    table = jnp.concatenate(
        [jnp.where(imaginary, -sine, cosine), jnp.where(imaginary, cosine, sine)], axis=1
    ).astype(jnp.bfloat16)
    lines = jnp.arange(2 * mode_count, dtype=jnp.int32)
    chosen = (lines[:, None] // 2) == ordered[None, :, 0]
    even = (lines % 2 == 0)[:, None]
    mask = jnp.concatenate([chosen & even, chosen & ~even], axis=1)
    return table, mask.astype(jnp.float32)


def group_size(snap_local, near):
    group = 1
    while snap_local % (2 * group) == 0 and 2 * group * near <= LANES - 2:
        group *= 2
    return group


def spectrum_kernel(x_ref, table_ref, mask_ref, out_ref, held):
    block, lines, points = x_ref.shape
    columns = out_ref.shape[0]
    held[...] = jnp.zeros_like(held)
    for start in range(0, block, CHUNK):
        rows = x_ref[start:start + CHUNK].reshape(CHUNK * lines, points)
        product = jnp.dot(rows, table_ref[...], preferred_element_type=jnp.float32)
        product = product.reshape(CHUNK, lines, 2 * columns) * mask_ref[...][None]
        both = product[:, :, :columns] + product[:, :, columns:]
        held[start:start + CHUNK, :] = jnp.sum(both, axis=1)
    out_ref[:, pl.ds(pl.program_id(0), 1), :] = held[...].T[:, None, :]


def spectrum(values, table, mask, near, group):
    lines, points = values.shape[1:]
    columns = mask.shape[1] // 2
    block = near * group
    steps = values.shape[0] // block
    return pl.pallas_call(
        spectrum_kernel,
        grid=(steps,),
        in_specs=[pl.BlockSpec((block, lines, points), lambda i: (i, 0, 0)),
                  pl.BlockSpec(table.shape, lambda i: (0, 0)),
                  pl.BlockSpec(mask.shape, lambda i: (0, 0))],
        out_specs=pl.BlockSpec((columns, steps, LANES), lambda i: (0, 0, 0)),
        out_shape=jax.ShapeDtypeStruct((columns, steps, LANES), jnp.float32),
        scratch_shapes=[pltpu.VMEM((LANES, columns), jnp.float32)],
        cost_estimate=pl.CostEstimate(flops=4 * values.size * columns, bytes_accessed=2 * values.size, transcendentals=0),
    )(values, table, mask)


def gather_pair(ref, pair, near, group):
    snap_count, height_count, _, _, steps, _ = ref.shape
    lane = lax.broadcasted_iota(jnp.int32, (1, LANES), 1)
    pieces = []
    for height in range(height_count):
        parts = []
        for half in range(2):
            block = ref[:, height, pair, half].reshape(snap_count * steps, LANES)
            for member in range(group):
                moved = block if member == 0 else pltpu.roll(block, LANES - member * near, 1)
                parts.append(jnp.where(lane < near, moved, 0.0))
        pieces.append(jnp.concatenate(parts, axis=0))
    return jnp.concatenate(pieces, axis=1)


def invert_kernel(near, group, ridge_ref, x_ref, smooth_ref):
    pairs = x_ref.shape[2]
    snaps = smooth_ref.shape[1] // 2
    lane = lax.broadcasted_iota(jnp.int32, (snaps, 2 * snaps), 1)
    line = lax.broadcasted_iota(jnp.int32, (snaps, 2 * snaps), 0)
    sign = jnp.where(lax.broadcasted_iota(jnp.int32, (1, 2 * snaps), 1) < snaps, -1.0, 1.0)

    def embed(top):
        return jnp.concatenate([top, pltpu.roll(top, snaps, 1) * sign], axis=0)

    grams = []
    states = []
    for pair in range(pairs):
        stacked = gather_pair(x_ref, pair, near, group)
        gram = lax.dot_general(stacked, stacked, (((1,), (1,)), ((), ())), precision=HIGHEST,
                               preferred_element_type=jnp.float32)
        swapped = pltpu.roll(gram[snaps:], snaps, 1)
        top = gram[:snaps] + jnp.where(lane < snaps, swapped, 0.0)
        top = jnp.where(lane < snaps, top, swapped - gram[:snaps])
        grams.append(top)
        states.append(top + jnp.where(line == lane, ridge_ref[pair], 0.0))
    turned = [pltpu.roll(state, snaps, 1) * sign for state in states]
    for k in range(snaps):
        here = line == k
        column = (lane == k) | (lane == snaps + k)
        unit = jnp.where(here & (lane == k), 1.0, 0.0)
        other = jnp.where(here & (lane == snaps + k), 1.0, 0.0)
        for pair in range(pairs):
            state, twin = states[pair], turned[pair]
            first = state[:, k:k + 1]
            second = state[:, snaps + k:snaps + k + 1]
            inverse = 1.0 / state[k:k + 1, k:k + 1]
            cleared = jnp.where(column, unit, state)
            cleared_twin = jnp.where(column, other, twin)
            row = cleared[k:k + 1, :] * inverse
            row_twin = cleared_twin[k:k + 1, :] * inverse
            states[pair] = jnp.where(here, row, cleared - (first * row + second * row_twin))
            turned[pair] = jnp.where(here, row_twin, cleared_twin - (first * row_twin - second * row))
    for pair in range(pairs):
        smooth_ref[pair] = jnp.dot(embed(grams[pair]), jnp.concatenate([states[pair], turned[pair]], axis=0), precision=HIGHEST,
                                   preferred_element_type=jnp.float32)


def apply_kernel(near, group, smooth_ref, y_ref, back_ref):
    snap_count, height_count, pairs, _, steps, _ = y_ref.shape
    members = snap_count * steps
    half_rows = group * members
    lane = lax.broadcasted_iota(jnp.int32, (1, LANES), 1)
    misses = jnp.zeros((1, 1), jnp.float32)
    energy = jnp.zeros((1, 1), jnp.float32)
    for pair in range(pairs):
        target = gather_pair(y_ref, pair, near, group)
        fitted = jnp.dot(smooth_ref[pair], target, precision=HIGHEST, preferred_element_type=jnp.float32)
        gap = target - fitted
        misses = misses + jnp.sum(gap * gap, keepdims=True)
        energy = energy + jnp.sum(target * target, keepdims=True)
        note = jnp.where(lane == near * group, misses, jnp.where(lane == near * group + 1, energy, 0.0))
        for height in range(height_count):
            for half in range(2):
                block = jnp.broadcast_to(note, (members, LANES))
                for member in range(group):
                    start = half * half_rows + member * members
                    piece = fitted[start:start + members, height * LANES:(height + 1) * LANES]
                    block = block + (piece if member == 0 else pltpu.roll(piece, member * near, 1))
                back_ref[:, height, pair, half] = block.reshape(snap_count, steps, LANES)


def finish_kernel(near, group, back_ref, predicted_ref, misfit_ref):
    owners, pairs, _, steps, _ = back_ref.shape
    block = near * group
    for half in range(2):
        for step in range(steps):
            sheet = back_ref[:, :, half, step, :].reshape(owners * pairs, LANES)
            predicted_ref[step * block:(step + 1) * block, half, :] = sheet.T[:block]
    notes = jnp.sum(back_ref[:, pairs - 1, 0, 0, :], axis=0, keepdims=True)
    misfit_ref[...] = notes[:, block:block + 1] / notes[:, block + 1:block + 2]


def exchange(message):
    return lax.all_to_all(message, ("snap", "height"), split_axis=0, concat_axis=0, tiled=True)


def scatter_kernel(out_ref, in_ref, send_sem, recv_sem, own_sem):
    owners = out_ref.shape[0]
    height_count = lax.axis_size("height")
    me = lax.axis_index("snap") * height_count + lax.axis_index("height")
    barrier = pltpu.get_barrier_semaphore()

    def peer(step):
        other = lax.rem(me + step, owners)
        return other, (other // height_count, lax.rem(other, height_count))

    def greet(step, carry):
        _, where = peer(step)
        pl.semaphore_signal(barrier, inc=1, device_id=where, device_id_type=pl.DeviceIdType.MESH)
        return carry

    def copy(step):
        other, where = peer(step)
        return pltpu.make_async_remote_copy(
            src_ref=out_ref.at[other],
            dst_ref=in_ref.at[me],
            send_sem=send_sem.at[step],
            recv_sem=recv_sem.at[step],
            device_id=where,
            device_id_type=pl.DeviceIdType.MESH,
        )

    def start(step, carry):
        copy(step).start()
        return carry

    def finish(step, carry):
        copy(step).wait()
        return carry

    own = pltpu.make_async_copy(out_ref.at[me], in_ref.at[me], own_sem)
    own.start()
    lax.fori_loop(1, owners, greet, 0)
    pl.semaphore_wait(barrier, owners - 1)
    lax.fori_loop(1, owners, start, 0)
    lax.fori_loop(1, owners, finish, 0)
    own.wait()


def scatter(message):
    owners = message.shape[0]
    vmem = pl.BlockSpec(memory_space=pltpu.VMEM)
    return pl.pallas_call(
        scatter_kernel,
        in_specs=[vmem],
        out_specs=vmem,
        out_shape=jax.ShapeDtypeStruct(message.shape, message.dtype),
        scratch_shapes=[pltpu.SemaphoreType.DMA((owners,)), pltpu.SemaphoreType.DMA((owners,)),
                        pltpu.SemaphoreType.DMA],
        compiler_params=pltpu.CompilerParams(collective_id=0, has_side_effects=True),
    )(message)


def per_device(resolved, drain, pair_list, ridge_index):
    snap_local, components, height_local, mode_count, halves, points = resolved.shape
    snap_count = lax.axis_size("snap")
    height_count = lax.axis_size("height")
    owners = snap_count * height_count
    pair_total = pair_list.shape[0]
    pair_local = pair_total // owners
    near = components * height_local
    rows = snap_local * near
    snaps = snap_count * snap_local
    group = group_size(snap_local, near)
    steps = snap_local // group
    sent = (owners, pair_local, 2, steps, LANES)
    held = (snap_count, height_count, pair_local, 2, steps, LANES)
    vmem = pl.BlockSpec(memory_space=pltpu.VMEM)
    smem = pl.BlockSpec(memory_space=pltpu.SMEM)

    table, mask = pair_tables(pair_list, points, mode_count)
    spec_x = spectrum(resolved.reshape(rows, -1, points), table, mask, near, group)
    arrived_x = exchange(spec_x.reshape(sent))
    spec_y = spectrum(drain.reshape(rows, -1, points), table, mask, near, group)
    arrived_y = exchange(spec_y.reshape(sent))
    owner_index = lax.axis_index("snap") * height_count + lax.axis_index("height")
    levels = lax.dynamic_slice_in_dim(ridge_index, owner_index * pair_local, pair_local, 0)
    ridge = 0.25 * jnp.exp2(levels.astype(jnp.float32)) * snaps
    smooth = pl.pallas_call(
        functools.partial(invert_kernel, near, group),
        in_specs=[smem, vmem],
        out_specs=vmem,
        out_shape=jax.ShapeDtypeStruct((pair_local, 2 * snaps, 2 * snaps), jnp.float32),
        cost_estimate=pl.CostEstimate(flops=10**10, bytes_accessed=2**20, transcendentals=0),
    )(ridge, arrived_x.reshape(held))
    back = pl.pallas_call(
        functools.partial(apply_kernel, near, group),
        in_specs=[vmem, vmem],
        out_specs=vmem,
        out_shape=jax.ShapeDtypeStruct(held, jnp.float32),
    )(smooth, arrived_y.reshape(held))
    returned = scatter(back.reshape(sent))
    predicted, misfit = pl.pallas_call(
        functools.partial(finish_kernel, near, group),
        in_specs=[vmem],
        out_specs=[vmem, vmem],
        out_shape=[jax.ShapeDtypeStruct((rows, 2, pair_total), jnp.float32),
                   jax.ShapeDtypeStruct((1, 1), jnp.float32)],
    )(returned)
    predicted = predicted.reshape(snap_local, components, height_local, 2, pair_total)
    return (predicted, misfit.reshape(1))


def solution(mesh):
    return jax.shard_map(
        per_device,
        mesh=mesh,
        in_specs=(
            P("snap", None, "height", None, None, None),
            P("snap", None, "height", None, None, None),
            P(),
            P(),
        ),
        out_specs=(P("snap", None, "height", None, None), P()),
        check_vma=False,
    )
```

profile of v0, /device:TPU:0, one launch (start us, length us, event | category | flops | bytes accessed | tf_op | source)
XLA Modules:
  0.0 78.6 jit_solution(4786091688782382891)
XLA Ops:
  0.7 0.8 broadcast_in_dim.21
  1.4 0.1 reshape.98
  1.6 0.1 compare_and_fusion.1
  1.7 0.6 add_convert_fusion.mask_ref
  2.3 0.3 select_convert_fusion.1
  2.6 0.6 pad_maximum_fusion.table_ref
  3.2 0.0 copy-start.2
  3.2 8.8 %shard_map.59 = f32[128,8,128]{2,1,0:T(8,128)} custom-call(bf16[768,32,128]{2,1,0:T(8,128)(2,1)} %bitcast.15, bf16[128,256]{1,0:T(8,128)(2,1)} %pad_maximum_fusion.table_ref, f32[32,256]{1,0:T(8,128)} %add_convert_fusion.mask_ref), custom_call_target="tpu_custom_call" | custom-call | flops 1610612736 | bytes 6291456 | tf_op jit(solution)/shard_map/pallas_call | solution.py:60
  12.0 7.3 %all-to-all-start = ((f32[32,2,2,8,128]{4,3,2,1,0:T(8,128)}), f32[32,2,2,8,128]{4,3,2,1,0:T(8,128)S(1)}, u32[]{:S(2)}, u32[]{:S(2)}) async-start(f32[32,2,2,8,128]{4,3,2,1,0:T(8,128)} %bitcast.19), calls=%async_computation | async-start | bytes 1048576 | tf_op jit(solution)/shard_map/all_to_all | solution.py:167
  19.3 8.8 %shard_map.61 = f32[128,8,128]{2,1,0:T(8,128)} custom-call(bf16[768,32,128]{2,1,0:T(8,128)(2,1)} %bitcast.16, bf16[128,256]{1,0:T(8,128)(2,1)} %pad_maximum_fusion.table_ref, f32[32,256]{1,0:T(8,128)} %add_convert_fusion.mask_ref), custom_call_target="tpu_custom_call" | custom-call | flops 1610612736 | bytes 6291456 | tf_op jit(solution)/shard_map/pallas_call | solution.py:60
  28.1 7.5 %all-to-all-done = f32[32,2,2,8,128]{4,3,2,1,0:T(8,128)S(1)} async-done(((f32[32,2,2,8,128]{4,3,2,1,0:T(8,128)}), f32[32,2,2,8,128]{4,3,2,1,0:T(8,128)S(1)}, u32[]{:S(2)}, u32[]{:S(2)}) %all-to-all-start) | async-done | bytes 524320 | tf_op jit(solution)/shard_map/all_to_all | solution.py:167
  35.7 0.0 copy-start.1
  35.7 2.6 %all-to-all-start.1 = ((f32[32,2,2,8,128]{4,3,2,1,0:T(8,128)}), f32[32,2,2,8,128]{4,3,2,1,0:T(8,128)S(1)}, u32[]{:S(2)}, u32[]{:S(2)}) async-start(f32[32,2,2,8,128]{4,3,2,1,0:T(8,128)} %bitcast.20), calls=%async_computation.1 | async-start | bytes 1048576 | tf_op jit(solution)/shard_map/all_to_all | solution.py:167
  38.3 0.0 copy-done.2
  38.3 0.6 exponential_multiply_fusion.ridge_ref
  38.9 0.0 copy-done.1
  38.9 9.3 %shard_map.60.smooth_ref = f32[2,128,128]{2,1,0:T(8,128)} custom-call(f32[2]{0:T(128)} %exponential_multiply_fusion.ridge_ref, f32[4,8,2,2,8,128]{5,4,3,2,1,0:T(8,128)} %bitcast.21), custom_call_target="tpu_custom_call" | custom-call | flops 10000000000 | bytes 1048576 | tf_op jit(solution)/shard_map/pallas_call | solution.py:252
  48.2 6.5 %all-to-all-done.1 = f32[32,2,2,8,128]{4,3,2,1,0:T(8,128)S(1)} async-done(((f32[32,2,2,8,128]{4,3,2,1,0:T(8,128)}), f32[32,2,2,8,128]{4,3,2,1,0:T(8,128)S(1)}, u32[]{:S(2)}, u32[]{:S(2)}) %all-to-all-start.1) | async-done | bytes 524320 | tf_op jit(solution)/shard_map/all_to_all | solution.py:167
  54.6 0.0 copy-start
  54.6 0.8 %copy-done = f32[32,2,2,8,128]{4,3,2,1,0:T(8,128)} copy-done((f32[32,2,2,8,128]{4,3,2,1,0:T(8,128)}, f32[32,2,2,8,128]{4,3,2,1,0:T(8,128)S(1)}, u32[]{:S(2)}) %copy-start) | copy-done | bytes 524312
  55.4 3.3 %shard_map.62 = f32[4,8,2,2,8,128]{5,4,3,2,1,0:T(8,128)} custom-call(f32[2,128,128]{2,1,0:T(8,128)} %shard_map.60.smooth_ref, f32[4,8,2,2,8,128]{5,4,3,2,1,0:T(8,128)} %bitcast.17), custom_call_target="tpu_custom_call" | custom-call | tf_op jit(solution)/shard_map/pallas_call | solution.py:259
  58.7 17.3 %shard_map.63.back_ref = f32[32,2,2,8,128]{4,3,2,1,0:T(8,128)} custom-call(f32[32,2,2,8,128]{4,3,2,1,0:T(8,128)} %bitcast.18), custom_call_target="tpu_custom_call" | custom-call | tf_op jit(solution)/shard_map/pallas_call | solution.py:216
  76.0 2.6 %shard_map.64 = (f32[768,2,64]{2,1,0:T(2,128)}, f32[1,1]{1,0:T(1,128)}) custom-call(f32[32,2,2,8,128]{4,3,2,1,0:T(8,128)} %shard_map.63.back_ref), custom_call_target="tpu_custom_call" | custom-call | tf_op jit(solution)/shard_map/pallas_call | solution.py:266
  (4 shorter events, 0.0 us)
Async XLA Ops:
  3.2 35.1 %copy-start.2 = (s32[64]{0:T(128)S(1)}, s32[64]{0:T(128)}, u32[]{:S(2)}) copy-start(s32[64]{0:T(128)} %param.7) | copy-start | bytes 772
  12.0 23.7 %all-to-all-start = ((f32[32,2,2,8,128]{4,3,2,1,0:T(8,128)}), f32[32,2,2,8,128]{4,3,2,1,0:T(8,128)S(1)}, u32[]{:S(2)}, u32[]{:S(2)}) async-start(f32[32,2,2,8,128]{4,3,2,1,0:T(8,128)} %bitcast.19), calls=%async_computation | async-start | bytes 1048576 | tf_op jit(solution)/shard_map/all_to_all | solution.py:167
  35.7 3.2 %copy-start.1 = (f32[32,2,2,8,128]{4,3,2,1,0:T(8,128)}, f32[32,2,2,8,128]{4,3,2,1,0:T(8,128)S(1)}, u32[]{:S(2)}) copy-start(f32[32,2,2,8,128]{4,3,2,1,0:T(8,128)S(1)} %all-to-all-done) | copy-start | bytes 1572868
  35.7 19.0 %all-to-all-start.1 = ((f32[32,2,2,8,128]{4,3,2,1,0:T(8,128)}), f32[32,2,2,8,128]{4,3,2,1,0:T(8,128)S(1)}, u32[]{:S(2)}, u32[]{:S(2)}) async-start(f32[32,2,2,8,128]{4,3,2,1,0:T(8,128)} %bitcast.20), calls=%async_computation.1 | async-start | bytes 1048576 | tf_op jit(solution)/shard_map/all_to_all | solution.py:167
  54.6 0.8 %copy-start = (f32[32,2,2,8,128]{4,3,2,1,0:T(8,128)}, f32[32,2,2,8,128]{4,3,2,1,0:T(8,128)S(1)}, u32[]{:S(2)}) copy-start(f32[32,2,2,8,128]{4,3,2,1,0:T(8,128)S(1)} %all-to-all-done.1) | copy-start | bytes 1572868
where the time goes:
time: 79.3 us; the launch traced here: 78.6 us
  Pallas kernels  50.1 us (63%)
  waiting for transfers between devices  14 us (18%)
  starting transfers between devices  9.9 us (12%)
  other arithmetic  2.22 us (3%)
  local copies, waits for them, and re-layouts  1.71 us (2%)
    pallas_call x2, Pallas kernels, spectrum(): pl.pallas_call(spectrum_kernel, grid=(steps,), in_specs=[pl.BlockSpec((bl...  17.6 us
    pallas_call x1, Pallas kernels, scatter(): pl.pallas_call(scatter_kernel, in_specs=[vmem], out_specs=vmem, out_shape...  17.3 us
    all_to_all x2, waiting for transfers between devices, exchange(): lax.all_to_all(message, ('snap', 'height'), split_axis=0, concat_axis=0,...  14 us
    all_to_all x2, starting transfers between devices, exchange(): lax.all_to_all(message, ('snap', 'height'), split_axis=0, concat_axis=0,...  9.9 us
    pallas_call x1, Pallas kernels, per_device(): pl.pallas_call(functools.partial(invert_kernel, near, group), in_specs=[s...  9.29 us
    pallas_call x1, Pallas kernels, per_device(): pl.pallas_call(functools.partial(apply_kernel, near, group), in_specs=[vm...  3.29 us
    pallas_call x1, Pallas kernels, per_device(): pl.pallas_call(functools.partial(finish_kernel, near, group), in_specs=[v...  2.57 us
  transfers between devices with their start and end apart: 2, of which 2 were waited for; matrix products, arithmetic and copies ran while one was open for 1% of the time, Pallas kernels for 23%

commit v1 on v0

v1 whole, which is shorter than its diff:
```python
import functools
import math

import jax
import jax.numpy as jnp
import numpy as np
from jax import lax
from jax.experimental import pallas as pl
from jax.experimental.pallas import tpu as pltpu
from jax.sharding import PartitionSpec as P

HIGHEST = lax.Precision.HIGHEST
LANES = 128
TILE = 8
VMEM_BYTES = 48 << 20


def wave_table(points):
    grid = np.arange(points)
    theta = (grid[:, None] * grid[None, :] % points).astype(np.float32) * np.float32(2.0 * math.pi / points)
    scaling = np.float32(1.0 / math.sqrt(points))
    cosine = (np.cos(theta) * scaling).T
    sine = (np.sin(theta) * scaling).T
    rows = np.concatenate([np.concatenate([cosine, sine], 1), np.concatenate([-sine, cosine], 1)], 0)
    return rows.astype(jnp.bfloat16)


def round_up(value, unit):
    return -(-value // unit) * unit


def swap_groups(arrays, width):
    arrays = list(arrays)
    lane = lax.broadcasted_iota(jnp.int32, (1, LANES), 1)
    bit = 1
    while bit < len(arrays):
        low = (lane // width) % (2 * bit) < bit
        for index in range(len(arrays)):
            if index & bit:
                continue
            first, second = arrays[index], arrays[index + bit]
            arrays[index] = jnp.where(low, first, pltpu.roll(second, bit * width, 1))
            arrays[index + bit] = jnp.where(low, pltpu.roll(first, LANES - bit * width, 1), second)
        bit *= 2
    return arrays


def invert(gram, ridge):
    pairs = len(gram)
    snaps = gram[0].shape[0] // 2
    lane = lax.broadcasted_iota(jnp.int32, (snaps, 2 * snaps), 1)
    line = lax.broadcasted_iota(jnp.int32, (snaps, 2 * snaps), 0)
    sign = jnp.where(lax.broadcasted_iota(jnp.int32, (1, 2 * snaps), 1) < snaps, -1.0, 1.0)
    grams = []
    states = []
    for pair in range(pairs):
        whole = gram[pair]
        swapped = pltpu.roll(whole[snaps:], snaps, 1)
        top = whole[:snaps] + jnp.where(lane < snaps, swapped, 0.0)
        top = jnp.where(lane < snaps, top, swapped - whole[:snaps])
        grams.append(top)
        states.append(top + jnp.where(line == lane, ridge[pair], 0.0))
    turned = [pltpu.roll(state, snaps, 1) * sign for state in states]
    for k in range(snaps):
        here = line == k
        column = (lane == k) | (lane == snaps + k)
        unit = jnp.where(here & (lane == k), 1.0, 0.0)
        other = jnp.where(here & (lane == snaps + k), 1.0, 0.0)
        for pair in range(pairs):
            state, twin = states[pair], turned[pair]
            first = state[:, k:k + 1]
            second = state[:, snaps + k:snaps + k + 1]
            inverse = 1.0 / state[k:k + 1, k:k + 1]
            cleared = jnp.where(column, unit, state)
            cleared_twin = jnp.where(column, other, twin)
            row = cleared[k:k + 1, :] * inverse
            row_twin = cleared_twin[k:k + 1, :] * inverse
            states[pair] = jnp.where(here, row, cleared - (first * row + second * row_twin))
            turned[pair] = jnp.where(here, row_twin, cleared_twin - (first * row_twin - second * row))
    smooth = []
    for pair in range(pairs):
        full = jnp.concatenate([grams[pair], pltpu.roll(grams[pair], snaps, 1) * sign], axis=0)
        smooth.append(jnp.dot(full, jnp.concatenate([states[pair], turned[pair]], axis=0), precision=HIGHEST,
                              preferred_element_type=jnp.float32))
    return smooth


class Sizes:
    def __init__(self, shape, pair_total, snap_count, height_count):
        self.snap_local, self.components, self.height_local, self.modes, self.parts, self.points = shape
        self.snap_count, self.height_count = snap_count, height_count
        self.owners = snap_count * height_count
        self.pairs = pair_total
        self.pair_local = pair_total // self.owners
        self.near = self.components * self.height_local
        self.snaps = snap_count * self.snap_local
        self.groups = LANES // self.snap_local
        self.tiles = self.near // self.groups
        self.tiles_each = self.height_local // self.groups
        self.columns = 2 * self.pairs
        self.kinds = 2 * self.pair_local
        self.sent = self.tiles * self.kinds
        self.out_stride = round_up(self.sent, TILE)
        self.back = self.sent + 1
        self.back_stride = round_up(self.back, TILE)
        self.wide = self.modes * self.parts * self.points


def whole_kernel(z, wave_hbm, list_ref, ridge_ref, x_hbm, y_hbm, predicted_ref, misfit_ref,
                 wave, x_buf, y_buf, table, x_out, y_out, x_in, y_in, x_rows, y_rows, b_out, b_in,
                 load_sem, x_send, x_recv, y_send, y_recv, b_send, b_recv, own_sem):
    me = lax.axis_index("snap") * z.height_count + lax.axis_index("height")
    barrier = pltpu.get_barrier_semaphore()

    def peer(step):
        other = lax.rem(me + step, z.owners)
        return other, (other // z.height_count, lax.rem(other, z.height_count))

    def load(source, target, part, index):
        span = pl.ds(part * z.height_local, z.height_local)
        return pltpu.make_async_copy(source.at[:, span], target.at[:, span], load_sem.at[index])

    wave_copy = pltpu.make_async_copy(wave_hbm, wave, load_sem.at[0])
    wave_copy.start()
    x_loads = [load(x_hbm, x_buf, part, 1 + part) for part in range(z.components)]
    y_loads = [load(y_hbm, y_buf, part, 1 + z.components + part) for part in range(z.components)]
    for item in x_loads + y_loads:
        item.start()

    def greet(step, carry):
        _, where = peer(step)
        pl.semaphore_signal(barrier, inc=1, device_id=where, device_id_type=pl.DeviceIdType.MESH)
        return carry

    lax.fori_loop(1, z.owners, greet, 0)

    same = (lax.broadcasted_iota(jnp.int32, (z.pairs, z.pairs), 0)
            == lax.broadcasted_iota(jnp.int32, (z.pairs, z.pairs), 1))
    mode = jnp.sum(jnp.where(same, list_ref[0:1, :], 0), axis=1, keepdims=True)
    number = jnp.sum(jnp.where(same, list_ref[1:2, :], 0), axis=1, keepdims=True)
    mode = jnp.concatenate([mode, mode], axis=0)
    number = jnp.concatenate([number, number + z.points], axis=0)
    chosen = lax.broadcasted_iota(jnp.int32, (z.columns, 2 * z.points), 1) == number
    wave_copy.wait()
    picked = jnp.dot(jnp.where(chosen, 1.0, 0.0).astype(jnp.bfloat16), wave[...], preferred_element_type=jnp.float32)
    for index in range(z.modes):
        table[:, index * 2 * z.points:(index + 1) * 2 * z.points] = jnp.where(mode == index, picked, 0.0).astype(jnp.bfloat16)
    x_rows[...] = jnp.zeros_like(x_rows)
    y_rows[...] = jnp.zeros_like(y_rows)

    def spectrum(buf, loads, out):
        for part in range(z.components):
            loads[part].wait()
            rows = jnp.concatenate([buf[:, part * z.height_local + height].reshape(z.snap_local, z.wide)
                                    for height in range(z.height_local)], axis=0)
            product = lax.dot_general(table[...], rows, (((1,), (1,)), ((), ())), preferred_element_type=jnp.float32)
            for each in range(z.tiles_each):
                tile = part * z.tiles_each + each
                for kind in range(z.kinds):
                    out[pl.ds(tile * z.kinds + kind, z.owners, stride=z.out_stride), :] = (
                        product[kind * z.owners:(kind + 1) * z.owners, each * LANES:(each + 1) * LANES])

    def exchange(source, target, rows, stride, send, recv, own):
        def here(index):
            return pl.ds(pl.multiple_of(index * stride, TILE), rows)

        def copy(step):
            other, where = peer(step)
            return pltpu.make_async_remote_copy(
                src_ref=source.at[here(other)], dst_ref=target.at[here(me)], send_sem=send.at[step], recv_sem=recv.at[step],
                device_id=where, device_id_type=pl.DeviceIdType.MESH)

        kept = pltpu.make_async_copy(source.at[here(me)], target.at[here(me)], own_sem.at[own])

        def start():
            def one(step, carry):
                copy(step).start()
                return carry
            kept.start()
            lax.fori_loop(1, z.owners, one, 0)

        def finish():
            def one(step, carry):
                copy(step).wait()
                return carry
            lax.fori_loop(1, z.owners, one, 0)
            kept.wait()

        return start, finish

    x_start, x_finish = exchange(x_out, x_in, z.sent, z.out_stride, x_send, x_recv, 0)
    y_start, y_finish = exchange(y_out, y_in, z.sent, z.out_stride, y_send, y_recv, 1)
    b_start, b_finish = exchange(b_out, b_in, z.back, z.back_stride, b_send, b_recv, 2)

    spectrum(x_buf, x_loads, x_out)
    pl.semaphore_wait(barrier, z.owners - 1)
    x_start()
    spectrum(y_buf, y_loads, y_out)
    y_start()
    x_finish()

    sets = 2 * z.snap_count // z.groups

    def place(pair, height, index, stride):
        half, snap = index // z.snap_count, index % z.snap_count
        start = (snap * z.height_count + height) * stride + half * z.pair_local + pair
        return pl.ds(start, z.tiles, stride=z.kinds)

    def gather(source, target, pair):
        for height in range(z.height_count):
            for part in range(sets):
                moved = swap_groups([source[place(pair, height, part * z.groups + index, z.out_stride), :]
                                     for index in range(z.groups)], z.snap_local)
                for index, piece in enumerate(moved):
                    target[pair, pl.ds((height * z.groups + index) * TILE, z.tiles), part * LANES:(part + 1) * LANES] = piece

    gram = []
    ridge = []
    for pair in range(z.pair_local):
        gather(x_in, x_rows, pair)
        rows = x_rows[pair]
        gram.append(lax.dot_general(rows, rows, (((0,), (0,)), ((), ())), precision=HIGHEST, preferred_element_type=jnp.float32))
        mine = lax.broadcasted_iota(jnp.int32, (1, z.pairs), 1) == pair * z.owners + me
        level = jnp.sum(jnp.where(mine, ridge_ref[...], 0), axis=1, keepdims=True)
        ridge.append(lax.shift_left(jnp.ones_like(level), level).astype(jnp.float32) * (0.25 * z.snaps))
    smooth = invert(gram, ridge)

    y_finish()
    misses = jnp.zeros((1, 1), jnp.float32)
    energy = jnp.zeros((1, 1), jnp.float32)
    for pair in range(z.pair_local):
        gather(y_in, y_rows, pair)
        target = y_rows[pair]
        fitted = lax.dot_general(target, smooth[pair], (((1,), (1,)), ((), ())), precision=HIGHEST,
                                 preferred_element_type=jnp.float32)
        gap = target - fitted
        misses = misses + jnp.sum(gap * gap, keepdims=True)
        energy = energy + jnp.sum(target * target, keepdims=True)
        for height in range(z.height_count):
            for part in range(sets):
                moved = swap_groups([fitted[(height * z.groups + index) * TILE:(height * z.groups + index + 1) * TILE,
                                            part * LANES:(part + 1) * LANES] for index in range(z.groups)], z.snap_local)
                for index, piece in enumerate(moved):
                    b_out[place(pair, height, part * z.groups + index, z.back_stride), :] = piece[:z.tiles]
    lane = lax.broadcasted_iota(jnp.int32, (1, LANES), 1)
    note = jnp.where(lane == 0, misses, jnp.where(lane == 1, energy, 0.0))
    b_out[pl.ds(z.sent, z.owners, stride=z.back_stride), :] = jnp.broadcast_to(note, (z.owners, LANES))
    b_start()
    b_finish()

    for tile in range(z.tiles):
        for half in range(2):
            sheet = jnp.concatenate([b_in[pl.ds(tile * z.kinds + half * z.pair_local + pair, z.owners, stride=z.back_stride), :]
                                     for pair in range(z.pair_local)], axis=0)
            turned = sheet.T
            for index in range(z.groups):
                first = (tile * z.groups + index) * 2 + half
                block = turned[index * z.snap_local:(index + 1) * z.snap_local]
                if z.pairs <= LANES:
                    predicted_ref[pl.ds(first, z.snap_local, stride=2 * z.near), :] = block
                else:
                    for snap in range(z.snap_local):
                        predicted_ref[pl.ds(first + snap * 2 * z.near, 1), :] = block[snap:snap + 1]
    notes = jnp.sum(b_in[pl.ds(z.sent, z.owners, stride=z.back_stride), :], axis=0, keepdims=True)
    misfit_ref[...] = notes[:, 0:1] / notes[:, 1:2]


def per_device(resolved, drain, pair_list, ridge_index):
    z = Sizes(resolved.shape, pair_list.shape[0], lax.axis_size("snap"), lax.axis_size("height"))
    vmem = pl.BlockSpec(memory_space=pltpu.VMEM)
    hbm = pl.BlockSpec(memory_space=pltpu.HBM)
    block = (z.snap_local, z.near, z.modes * z.parts, z.points)
    out_rows = z.owners * z.out_stride
    back_rows = z.owners * z.back_stride
    gathered = (z.pair_local, z.height_count * z.groups * TILE, 2 * z.snaps)
    dma = pltpu.SemaphoreType.DMA((z.owners,))
    predicted, misfit = pl.pallas_call(
        functools.partial(whole_kernel, z),
        in_specs=[hbm, vmem, vmem, hbm, hbm],
        out_specs=[vmem, vmem],
        out_shape=[jax.ShapeDtypeStruct((z.snap_local * z.near * 2, z.pairs), jnp.float32),
                   jax.ShapeDtypeStruct((1, 1), jnp.float32)],
        scratch_shapes=[
            pltpu.VMEM((2 * z.points, 2 * z.points), jnp.bfloat16),
            pltpu.VMEM(block, jnp.bfloat16),
            pltpu.VMEM(block, jnp.bfloat16),
            pltpu.VMEM((z.columns, z.wide), jnp.bfloat16),
            pltpu.VMEM((out_rows, LANES), jnp.float32),
            pltpu.VMEM((out_rows, LANES), jnp.float32),
            pltpu.VMEM((out_rows, LANES), jnp.float32),
            pltpu.VMEM((out_rows, LANES), jnp.float32),
            pltpu.VMEM(gathered, jnp.float32),
            pltpu.VMEM(gathered, jnp.float32),
            pltpu.VMEM((back_rows, LANES), jnp.float32),
            pltpu.VMEM((back_rows, LANES), jnp.float32),
            pltpu.SemaphoreType.DMA((1 + 2 * z.components,)),
            dma, dma, dma, dma, dma, dma,
            pltpu.SemaphoreType.DMA((3,)),
        ],
        compiler_params=pltpu.CompilerParams(collective_id=0, has_side_effects=True, vmem_limit_bytes=VMEM_BYTES),
    )(jnp.asarray(wave_table(z.points)), pair_list.T, ridge_index.reshape(1, z.pairs), resolved.reshape(block), drain.reshape(block))
    predicted = predicted.reshape(z.snap_local, z.components, z.height_local, 2, z.pairs)
    return (predicted, misfit.reshape(1))


def solution(mesh):
    return jax.shard_map(
        per_device,
        mesh=mesh,
        in_specs=(
            P("snap", None, "height", None, None, None),
            P("snap", None, "height", None, None, None),
            P(),
            P(),
        ),
        out_specs=(P("snap", None, "height", None, None), P()),
        check_vma=False,
    )
```

time: 79.3 us -> 52 us (0.66)
  waiting for transfers between devices: 14 us -> 0 us
  starting transfers between devices: 9.9 us -> 0 us
  Pallas kernels: 50.1 us -> 46.3 us
  other arithmetic: 2.22 us -> 0 us
  between operations: 0.71 us -> 2.39 us
  local copies, waits for them, and re-layouts: 1.71 us -> 3.12 us
    all_to_all x2 -> x0, waiting for transfers between devices: 14 us -> none  [exchange(): lax.all_to_all(message, ('snap', 'height'), split_axis=0, concat_axis=0,...]
    all_to_all x2 -> x0, starting transfers between devices: 9.9 us -> none  [exchange(): lax.all_to_all(message, ('snap', 'height'), split_axis=0, concat_axis=0,...]
    pallas_call x6 -> x1, Pallas kernels: 50.1 us -> 46.3 us  [per_device(): pl.pallas_call(functools.partial(whole_kernel, z), in_specs=[hbm, vmem, v...]
    unnamed x6 -> x7, local copies, waits for them, and re-layouts: 0.8 us -> 3.12 us
  transfers between devices with their start and end apart: 2 -> 0, of which waited for: 2 -> 0; matrix products, arithmetic and copies ran while one was open for 1% -> 0% of each run, Pallas kernels for 23% -> 0%
where the time goes in v1:
time: 52 us; the launch traced here: 51.8 us
  Pallas kernels  46.3 us (89%)
  local copies, waits for them, and re-layouts  3.12 us (6%)
  between operations  2.39 us (5%)
    pallas_call x1, Pallas kernels, per_device(): pl.pallas_call(functools.partial(whole_kernel, z), in_specs=[hbm, vmem, v...  46.3 us
    unnamed x7, local copies, waits for them, and re-layouts  3.12 us

profile of v1, /device:TPU:0, one launch (start us, length us, event | category | flops | bytes accessed | tf_op | source)
XLA Modules:
  0.0 51.8 jit_solution(605027218344825653)
XLA Ops:
  0.6 0.0 copy-start
  0.6 0.9 %copy-done = bf16[256,256]{1,0:T(8,128)(2,1)S(1)} copy-done((bf16[256,256]{1,0:T(8,128)(2,1)S(1)}, bf16[256,256]{1,0:T(8,128)(2,1)}, u32[]{:S(2)}) %copy-start) | copy-done | bytes 131096
  1.5 0.0 copy-start.1
  1.5 0.7 %copy-done.1 = s32[64,2]{0,1:T(2,128)S(1)} copy-done((s32[64,2]{0,1:T(2,128)S(1)}, s32[64,2]{0,1:T(2,128)}, u32[]{:S(2)}) %copy-start.1) | copy-done | bytes 536
  2.2 0.0 copy-start.2
  2.2 0.7 %copy-done.2 = s32[64]{0:T(128)S(1)} copy-done((s32[64]{0:T(128)S(1)}, s32[64]{0:T(128)}, u32[]{:S(2)}) %copy-start.2) | copy-done | bytes 280
  2.9 46.3 %shard_map.68 = (f32[1536,64]{1,0:T(8,128)S(1)}, f32[1,1]{1,0:T(1,128)}) custom-call(bf16[256,256]{1,0:T(8,128)(2,1)S(1)} %copy-done, s32[2,64]{1,0:T(2,128)S(1)} %bitcast.7, s32[1,64]{1,0:T(1,128)S(1)} %bitcast.8, bf16[16,48,32,128]{3,2,1,0:T(8,128)(2,1)} %bitcast.9, bf16[16,48,32,128]{3,2,1,0:T(8,128)(2,1)} %bitcast.10), custom_call_target="tpu_custom_call" | custom-call | tf_op jit(solution)/shard_map/pallas_call | solution.py:277
  49.2 0.9 %copy.9 = f32[16,3,16,2,64]{4,3,2,1,0:T(2,128)} copy(f32[16,3,16,2,64]{4,3,2,1,0:T(2,128)S(1)} %bitcast.6) | data formatting | bytes 786432
Async XLA Ops:
  0.6 0.9 %copy-start = (bf16[256,256]{1,0:T(8,128)(2,1)S(1)}, bf16[256,256]{1,0:T(8,128)(2,1)}, u32[]{:S(2)}) copy-start(bf16[256,256]{1,0:T(8,128)(2,1)} %constant.2.clone.wave_hbm) | copy-start | bytes 393220
  1.5 0.7 %copy-start.1 = (s32[64,2]{0,1:T(2,128)S(1)}, s32[64,2]{0,1:T(2,128)}, u32[]{:S(2)}) copy-start(s32[64,2]{0,1:T(2,128)} %param.7) | copy-start | bytes 1540
  2.2 0.7 %copy-start.2 = (s32[64]{0:T(128)S(1)}, s32[64]{0:T(128)}, u32[]{:S(2)}) copy-start(s32[64]{0:T(128)} %param.8) | copy-start | bytes 772

commit v2 on v1

v2 whole, which is shorter than its diff:
```python
import functools
import math

import jax
import jax.numpy as jnp
import numpy as np
from jax import lax
from jax.experimental import pallas as pl
from jax.experimental.pallas import tpu as pltpu
from jax.sharding import PartitionSpec as P

HIGHEST = lax.Precision.HIGHEST
LANES = 128
TILE = 8
VMEM_BYTES = 48 << 20


def wave_table(points):
    grid = np.arange(points)
    theta = (grid[:, None] * grid[None, :] % points).astype(np.float32) * np.float32(2.0 * math.pi / points)
    scaling = np.float32(1.0 / math.sqrt(points))
    cosine = (np.cos(theta) * scaling).T
    sine = (np.sin(theta) * scaling).T
    rows = np.concatenate([np.concatenate([cosine, sine], 1), np.concatenate([-sine, cosine], 1)], 0)
    return rows.astype(jnp.bfloat16)


def round_up(value, unit):
    return -(-value // unit) * unit


def swap_groups(arrays, width):
    arrays = list(arrays)
    lane = lax.broadcasted_iota(jnp.int32, (1, LANES), 1)
    bit = 1
    while bit < len(arrays):
        low = (lane // width) % (2 * bit) < bit
        for index in range(len(arrays)):
            if index & bit:
                continue
            first, second = arrays[index], arrays[index + bit]
            arrays[index] = jnp.where(low, first, pltpu.roll(second, bit * width, 1))
            arrays[index + bit] = jnp.where(low, pltpu.roll(first, LANES - bit * width, 1), second)
        bit *= 2
    return arrays


def invert(gram, ridge):
    pairs = len(gram)
    snaps = gram[0].shape[0] // 2
    lane = lax.broadcasted_iota(jnp.int32, (snaps, 2 * snaps), 1)
    line = lax.broadcasted_iota(jnp.int32, (snaps, 2 * snaps), 0)
    sign = jnp.where(lax.broadcasted_iota(jnp.int32, (1, 2 * snaps), 1) < snaps, -1.0, 1.0)
    grams = []
    states = []
    for pair in range(pairs):
        whole = gram[pair]
        swapped = pltpu.roll(whole[snaps:], snaps, 1)
        top = whole[:snaps] + jnp.where(lane < snaps, swapped, 0.0)
        top = jnp.where(lane < snaps, top, swapped - whole[:snaps])
        grams.append(top)
        states.append(top + jnp.where(line == lane, ridge[pair], 0.0))
    turned = [pltpu.roll(state, snaps, 1) * sign for state in states]
    for k in range(0, snaps, 2):
        near, far = line == k, line == k + 1
        column = (lane // 2 == k // 2) | (lane // 2 == (snaps + k) // 2)
        unit = jnp.where((near | far) & (lane == line), 1.0, 0.0)
        other = jnp.where((near | far) & (lane == snaps + line), 1.0, 0.0)
        for pair in range(pairs):
            state, twin = states[pair], turned[pair]
            first_re, second_re = state[:, k:k + 1], state[:, k + 1:k + 2]
            first_im, second_im = state[:, snaps + k:snaps + k + 1], state[:, snaps + k + 1:snaps + k + 2]
            head, tail = state[k:k + 1, k:k + 1], state[k + 1:k + 2, k + 1:k + 2]
            cross_re, cross_im = state[k:k + 1, k + 1:k + 2], state[k:k + 1, snaps + k + 1:snaps + k + 2]
            inverse = 1.0 / (head * tail - (cross_re * cross_re + cross_im * cross_im))
            head, tail, cross_re, cross_im = head * inverse, tail * inverse, cross_re * inverse, cross_im * inverse
            cleared = jnp.where(column, unit, state)
            cleared_twin = jnp.where(column, other, twin)
            one, two = cleared[k:k + 1, :], cleared[k + 1:k + 2, :]
            one_twin, two_twin = cleared_twin[k:k + 1, :], cleared_twin[k + 1:k + 2, :]
            top = tail * one - (cross_re * two + cross_im * two_twin)
            top_twin = tail * one_twin - (cross_re * two_twin - cross_im * two)
            low = head * two - (cross_re * one - cross_im * one_twin)
            low_twin = head * two_twin - (cross_re * one_twin + cross_im * one)
            fresh = cleared - ((first_re * top + first_im * top_twin) + (second_re * low + second_im * low_twin))
            fresh_twin = cleared_twin - ((first_re * top_twin - first_im * top) + (second_re * low_twin - second_im * low))
            states[pair] = jnp.where(near, top, jnp.where(far, low, fresh))
            turned[pair] = jnp.where(near, top_twin, jnp.where(far, low_twin, fresh_twin))
    return [jnp.dot(grams[pair], jnp.concatenate([states[pair], turned[pair]], axis=0), precision=HIGHEST,
                    preferred_element_type=jnp.float32) for pair in range(pairs)]


class Sizes:
    def __init__(self, shape, pair_total, snap_count, height_count):
        self.snap_local, self.components, self.height_local, self.modes, self.parts, self.points = shape
        self.snap_count, self.height_count = snap_count, height_count
        self.owners = snap_count * height_count
        self.pairs = pair_total
        self.pair_local = pair_total // self.owners
        self.near = self.components * self.height_local
        self.snaps = snap_count * self.snap_local
        self.groups = LANES // self.snap_local
        self.tiles = self.near // self.groups
        self.tiles_each = self.height_local // self.groups
        self.columns = 2 * self.pairs
        self.kinds = 2 * self.pair_local
        self.sent = self.tiles * self.kinds
        self.out_stride = round_up(self.sent, TILE)
        self.back = self.sent + 1
        self.back_stride = round_up(self.back, TILE)
        self.wide = self.modes * self.parts * self.points
        self.half_heights = height_count // 2
        self.half_owners = snap_count * self.half_heights
        self.sets = 2 * snap_count // self.groups


def embed(top):
    snaps = top.shape[0]
    sign = jnp.where(lax.broadcasted_iota(jnp.int32, (1, 2 * snaps), 1) < snaps, -1.0, 1.0)
    return jnp.concatenate([top, pltpu.roll(top, snaps, 1) * sign], axis=0)


def whole_kernel(z, wave_hbm, list_hbm, ridge_hbm, x_hbm, y_hbm, predicted_ref, misfit_ref,
                 wave, list_ref, ridge_ref, x_buf, y_buf, table, x_out, y_out, x_in, y_in, x_rows, y_rows, s_out, s_in,
                 b_out, b_in, note_out, note_in,
                 load_sem, x_send, x_recv, y_send, y_recv, s_send, s_recv, b_send, b_recv, note_send, note_recv, own_sem):
    snap, height = lax.axis_index("snap"), lax.axis_index("height")
    half, inner = height // z.half_heights, lax.rem(height, z.half_heights)
    own_slot = snap * z.height_count + inner * 2 + half
    twin_slot = snap * z.height_count + inner * 2 + (1 - half)
    barrier = pltpu.get_barrier_semaphore()

    def wrap(value, count):
        return lax.rem(value + count, count)

    def slot_of(snap_at, height_at):
        return snap_at * z.height_count + lax.rem(height_at, z.half_heights) * 2 + height_at // z.half_heights

    def away(step):
        return wrap(snap + lax.rem(step, z.snap_count), z.snap_count), wrap(height + step // z.snap_count, z.height_count)

    def beside(step, sign, side):
        return (wrap(snap + sign * lax.rem(step, z.snap_count), z.snap_count),
                side * z.half_heights + wrap(inner + sign * (step // z.snap_count), z.half_heights))

    def load(source, target, part, index):
        span = pl.ds(part * z.height_local, z.height_local)
        return pltpu.make_async_copy(source.at[:, span], target.at[:, span], load_sem.at[index])

    small = [pltpu.make_async_copy(source, target, load_sem.at[2 * z.components + index])
             for index, (source, target) in enumerate([(list_hbm, list_ref), (wave_hbm, wave), (ridge_hbm, ridge_ref)])]
    for item in small:
        item.start()
    x_loads = [load(x_hbm, x_buf, part, part) for part in range(z.components)]
    y_loads = [load(y_hbm, y_buf, part, z.components + part) for part in range(z.components)]
    for item in x_loads + y_loads:
        item.start()

    def greet(step, carry):
        pl.semaphore_signal(barrier, inc=1, device_id=away(step), device_id_type=pl.DeviceIdType.MESH)
        return carry

    lax.fori_loop(1, z.owners, greet, 0)

    same = (lax.broadcasted_iota(jnp.int32, (z.pairs, z.pairs), 0)
            == lax.broadcasted_iota(jnp.int32, (z.pairs, z.pairs), 1))
    small[0].wait()
    mode = jnp.sum(jnp.where(same, list_ref[0:1, :], 0), axis=1, keepdims=True)
    number = jnp.sum(jnp.where(same, list_ref[1:2, :], 0), axis=1, keepdims=True)
    mode = jnp.concatenate([mode, mode], axis=0)
    number = jnp.concatenate([number, number + z.points], axis=0)
    chosen = lax.broadcasted_iota(jnp.int32, (z.columns, 2 * z.points), 1) == number
    small[1].wait()
    picked = jnp.dot(jnp.where(chosen, 1.0, 0.0).astype(jnp.bfloat16), wave[...], preferred_element_type=jnp.float32)
    for index in range(z.modes):
        table[:, index * 2 * z.points:(index + 1) * 2 * z.points] = jnp.where(mode == index, picked, 0.0).astype(jnp.bfloat16)
    x_rows[...] = jnp.zeros_like(x_rows)
    y_rows[...] = jnp.zeros_like(y_rows)

    def spectrum(buf, loads, out):
        for part in range(z.components):
            loads[part].wait()
            rows = jnp.concatenate([buf[:, part * z.height_local + index].reshape(z.snap_local, z.wide)
                                    for index in range(z.height_local)], axis=0)
            product = lax.dot_general(table[...], rows, (((1,), (1,)), ((), ())), preferred_element_type=jnp.float32)
            for each in range(z.tiles_each):
                tile = part * z.tiles_each + each
                for kind in range(z.kinds):
                    out[pl.ds(tile * z.kinds + kind, z.owners, stride=z.out_stride), :] = (
                        product[kind * z.owners:(kind + 1) * z.owners, each * LANES:(each + 1) * LANES])

    def at(index, stride, rows):
        return pl.ds(pl.multiple_of(index * stride, TILE), rows)

    def remote(source, target, send, recv, where):
        return pltpu.make_async_remote_copy(src_ref=source, dst_ref=target, send_sem=send, recv_sem=recv, device_id=where,
                                            device_id_type=pl.DeviceIdType.MESH)

    def each(copy, first, last, act):
        def one(step, carry):
            act(copy(step))
            return carry
        lax.fori_loop(first, last, one, 0)

    def start(item):
        item.start()

    def sent(item):
        item.wait_send()

    def arrived(item):
        item.wait_recv()

    def x_copy(step):
        where = away(step)
        return remote(x_out.at[at(slot_of(*where), z.out_stride, z.sent)], x_in.at[at(step, z.out_stride, z.sent)],
                      x_send.at[step], x_recv.at[step], where)

    def y_copy(step):
        where = beside(step, 1, half)
        first = where[0] * z.height_count + lax.rem(where[1], z.half_heights) * 2
        return remote(y_out.at[at(first, z.out_stride, 2 * z.out_stride)], y_in.at[at(step, 2 * z.out_stride, 2 * z.out_stride)],
                      y_send.at[step], y_recv.at[step], where)

    def b_copy(side, target):
        def copy(step):
            return remote(b_out.at[side, at(step, z.back_stride, z.back)], b_in.at[at(target, z.back_stride, z.back)],
                          b_send.at[side, step], b_recv.at[side, step], beside(step, -1, half))
        return copy

    def note_copy(step):
        return remote(note_out.at[pl.ds(0, 1)], note_in.at[at(step, TILE, 1)], note_send.at[step], note_recv.at[step],
                      beside(step, 1, 1 - half))

    x_kept = pltpu.make_async_copy(x_out.at[at(own_slot, z.out_stride, z.sent)], x_in.at[at(0, z.out_stride, z.sent)], own_sem.at[0])
    y_kept = pltpu.make_async_copy(
        y_out.at[at(snap * z.height_count + inner * 2, z.out_stride, 2 * z.out_stride)],
        y_in.at[at(0, 2 * z.out_stride, 2 * z.out_stride)], own_sem.at[1])
    slots = (own_slot, twin_slot)
    b_kept = [pltpu.make_async_copy(b_out.at[side, at(0, z.back_stride, z.back)], b_in.at[at(slots[side], z.back_stride, z.back)],
                                    own_sem.at[2 + side]) for side in range(2)]
    s_copy = remote(s_out, s_in, s_send, s_recv, (snap, (1 - half) * z.half_heights + inner))

    spectrum(x_buf, x_loads, x_out)
    pl.semaphore_wait(barrier, z.owners - 1)
    x_kept.start()
    each(x_copy, 1, z.owners, start)
    spectrum(y_buf, y_loads, y_out)
    y_kept.start()
    each(y_copy, 1, z.half_owners, start)

    def place(base, index, pair):
        part, member = index // z.snap_count, index % z.snap_count
        return base(member) + part * z.pair_local + pair

    def gather(source, base, pair, target, block):
        for group in range(z.sets):
            moved = swap_groups([source[pl.ds(place(base, group * z.groups + index, pair), z.tiles, stride=z.kinds), :]
                                 for index in range(z.groups)], z.snap_local)
            for index, piece in enumerate(moved):
                target[pl.ds((block * z.groups + index) * TILE, z.tiles), group * LANES:(group + 1) * LANES] = piece

    gram = [None] * z.pair_local
    batch = min(4, z.height_count)
    span = batch * z.groups * TILE
    for block in range(z.height_count):
        for member in range(z.snap_count):
            step = block * z.snap_count + member
            if step == 0:
                x_kept.wait()
            else:
                x_copy(step).wait_recv()
        for pair in range(z.pair_local):
            gather(x_in, lambda member: (block * z.snap_count + member) * z.out_stride, pair, x_rows.at[pair], block)
            if block % batch == batch - 1:
                rows = x_rows[pair, pl.ds((block // batch) * span, span), :]
                term = lax.dot_general(rows, rows, (((0,), (0,)), ((), ())), precision=HIGHEST, preferred_element_type=jnp.float32)
                gram[pair] = term if gram[pair] is None else gram[pair] + term
    small[2].wait()
    ridge = []
    for pair in range(z.pair_local):
        mine = lax.broadcasted_iota(jnp.int32, (1, z.pairs), 1) == pair * z.owners + own_slot
        level = jnp.sum(jnp.where(mine, ridge_ref[...], 0), axis=1, keepdims=True)
        ridge.append(lax.shift_left(jnp.ones_like(level), level).astype(jnp.float32) * (0.25 * z.snaps))
    tops = invert(gram, ridge)
    for pair in range(z.pair_local):
        s_out[pair] = tops[pair]
    s_copy.start()

    y_kept.wait()
    each(y_copy, 1, z.half_owners, arrived)
    lane = lax.broadcasted_iota(jnp.int32, (1, LANES), 1)

    def collect(side):
        which = half if side == 0 else 1 - half
        for pair in range(z.pair_local):
            for block in range(z.half_heights):
                gather(y_in, lambda member: ((block * z.snap_count + member) * 2 + which) * z.out_stride, pair,
                       y_rows.at[side, pair], block)

    def fit(side, tops):
        misses = jnp.zeros((1, 1), jnp.float32)
        energy = jnp.zeros((1, 1), jnp.float32)
        for pair in range(z.pair_local):
            target = y_rows[side, pair]
            fitted = lax.dot_general(target, embed(tops[pair]), (((1,), (1,)), ((), ())), precision=HIGHEST,
                                     preferred_element_type=jnp.float32)
            gap = target - fitted
            misses = misses + jnp.sum(gap * gap, keepdims=True)
            energy = energy + jnp.sum(target * target, keepdims=True)
            for block in range(z.half_heights):
                for group in range(z.sets):
                    moved = swap_groups([fitted[(block * z.groups + index) * TILE:(block * z.groups + index + 1) * TILE,
                                                group * LANES:(group + 1) * LANES] for index in range(z.groups)], z.snap_local)
                    for index, piece in enumerate(moved):
                        row = place(lambda member: (block * z.snap_count + member) * z.back_stride, group * z.groups + index, pair)
                        b_out[side, pl.ds(row, z.tiles, stride=z.kinds), :] = piece[:z.tiles]
        note = jnp.where(lane == 0, misses, jnp.where(lane == 1, energy, 0.0))
        for step in range(z.half_owners):
            b_out[side, pl.ds(step * z.back_stride + z.sent, 1), :] = note
        return note

    collect(0)
    note = fit(0, tops)
    b_kept[0].start()
    each(b_copy(0, own_slot), 1, z.half_owners, start)
    collect(1)
    s_copy.wait_recv()
    note = note + fit(1, [s_in[pair] for pair in range(z.pair_local)])
    b_kept[1].start()
    each(b_copy(1, twin_slot), 1, z.half_owners, start)
    note_out[...] = jnp.broadcast_to(note, note_out.shape)
    each(note_copy, 0, z.half_owners, start)

    each(x_copy, 1, z.owners, sent)
    each(y_copy, 1, z.half_owners, sent)
    s_copy.wait_send()
    for side in range(2):
        b_kept[side].wait()
        each(b_copy(side, slots[side]), 1, z.half_owners, arrived)
    each(note_copy, 0, z.half_owners, arrived)

    for tile in range(z.tiles):
        for part in range(2):
            sheet = jnp.concatenate([b_in[pl.ds(tile * z.kinds + part * z.pair_local + pair, z.owners, stride=z.back_stride), :]
                                     for pair in range(z.pair_local)], axis=0)
            turned = sheet.T
            for index in range(z.groups):
                first = (tile * z.groups + index) * 2 + part
                piece = turned[index * z.snap_local:(index + 1) * z.snap_local]
                if z.pairs <= LANES:
                    predicted_ref[pl.ds(first, z.snap_local, stride=2 * z.near), :] = piece
                else:
                    for line in range(z.snap_local):
                        predicted_ref[pl.ds(first + line * 2 * z.near, 1), :] = piece[line:line + 1]
    notes = (jnp.sum(b_in[pl.ds(z.sent, z.owners, stride=z.back_stride), :], axis=0, keepdims=True)
             + jnp.sum(note_in[pl.ds(0, z.half_owners, stride=TILE), :], axis=0, keepdims=True))
    misfit_ref[...] = notes[:, 0:1] / notes[:, 1:2]
    for side in range(2):
        each(b_copy(side, slots[side]), 1, z.half_owners, sent)
    each(note_copy, 0, z.half_owners, sent)


def per_device(resolved, drain, pair_list, ridge_index):
    z = Sizes(resolved.shape, pair_list.shape[0], lax.axis_size("snap"), lax.axis_size("height"))
    vmem = pl.BlockSpec(memory_space=pltpu.VMEM)
    hbm = pl.BlockSpec(memory_space=pltpu.HBM)
    block = (z.snap_local, z.near, z.modes * z.parts, z.points)
    out_rows = z.owners * z.out_stride
    back_rows = z.half_owners * z.back_stride
    gathered = z.groups * TILE
    dma = pltpu.SemaphoreType.DMA
    stay = functools.partial(pltpu.with_memory_space_constraint, memory_space=pltpu.HBM)
    predicted, misfit = pl.pallas_call(
        functools.partial(whole_kernel, z),
        in_specs=[hbm] * 5,
        out_specs=[vmem, vmem],
        out_shape=[jax.ShapeDtypeStruct((z.snap_local * z.near * 2, z.pairs), jnp.float32),
                   jax.ShapeDtypeStruct((1, 1), jnp.float32)],
        scratch_shapes=[
            pltpu.VMEM((2 * z.points, 2 * z.points), jnp.bfloat16),
            pltpu.VMEM((2, z.pairs), jnp.int32),
            pltpu.VMEM((1, z.pairs), jnp.int32),
            pltpu.VMEM(block, jnp.bfloat16),
            pltpu.VMEM(block, jnp.bfloat16),
            pltpu.VMEM((z.columns, z.wide), jnp.bfloat16),
            pltpu.VMEM((out_rows, LANES), jnp.float32),
            pltpu.VMEM((out_rows, LANES), jnp.float32),
            pltpu.VMEM((out_rows, LANES), jnp.float32),
            pltpu.VMEM((out_rows, LANES), jnp.float32),
            pltpu.VMEM((z.pair_local, z.height_count * gathered, 2 * z.snaps), jnp.float32),
            pltpu.VMEM((2, z.pair_local, z.half_heights * gathered, 2 * z.snaps), jnp.float32),
            pltpu.VMEM((z.pair_local, z.snaps, 2 * z.snaps), jnp.float32),
            pltpu.VMEM((z.pair_local, z.snaps, 2 * z.snaps), jnp.float32),
            pltpu.VMEM((2, back_rows, LANES), jnp.float32),
            pltpu.VMEM((2 * back_rows, LANES), jnp.float32),
            pltpu.VMEM((TILE, LANES), jnp.float32),
            pltpu.VMEM((z.half_owners * TILE, LANES), jnp.float32),
            dma((2 * z.components + 3,)),
            dma((z.owners,)), dma((z.owners,)),
            dma((z.half_owners,)), dma((z.half_owners,)),
            dma, dma,
            dma((2, z.half_owners)), dma((2, z.half_owners)),
            dma((z.half_owners,)), dma((z.half_owners,)),
            dma((4,)),
        ],
        compiler_params=pltpu.CompilerParams(collective_id=0, has_side_effects=True, vmem_limit_bytes=VMEM_BYTES),
    )(stay(jnp.asarray(wave_table(z.points))), stay(pair_list.T), stay(ridge_index.reshape(1, z.pairs)),
      resolved.reshape(block), drain.reshape(block))
    predicted = predicted.reshape(z.snap_local, z.components, z.height_local, 2, z.pairs)
    return (predicted, misfit.reshape(1))


def solution(mesh):
    return jax.shard_map(
        per_device,
        mesh=mesh,
        in_specs=(
            P("snap", None, "height", None, None, None),
            P("snap", None, "height", None, None, None),
            P(),
            P(),
        ),
        out_specs=(P("snap", None, "height", None, None), P()),
        check_vma=False,
    )
```

time: 52 us -> 49.6 us (0.954)
  local copies, waits for them, and re-layouts: 3.12 us -> 0.88 us
    unnamed x7 -> x1, local copies, waits for them, and re-layouts: 3.12 us -> 0.88 us
where the time goes in v2:
time: 49.6 us; the launch traced here: 49.4 us
  Pallas kernels  46.2 us (93%)
  between operations  2.33 us (5%)
  local copies, waits for them, and re-layouts  0.88 us (2%)
    pallas_call x1, Pallas kernels, per_device(): pl.pallas_call(functools.partial(whole_kernel, z), in_specs=[hbm] * 5, ou...  46.2 us

profile of v2, /device:TPU:0, one launch (start us, length us, event | category | flops | bytes accessed | tf_op | source)
XLA Modules:
  0.0 49.4 jit_solution(14816542052506882899)
XLA Ops:
  0.6 46.2 %shard_map.68 = (f32[1536,64]{1,0:T(8,128)S(1)}, f32[1,1]{1,0:T(1,128)}) custom-call(bf16[256,256]{1,0:T(8,128)(2,1)} %constant.2.clone.wave_hbm, s32[2,64]{1,0:T(2,128)} %bitcast.9, s32[1,64]{1,0:T(1,128)} %bitcast.10, bf16[16,48,32,128]{3,2,1,0:T(8,128)(2,1)} %bitcast.7, bf16[16,48,32,128]{3,2,1,0:T(8,128)(2,1)} %bitcast.8), custom_call_target="tpu_custom_call" | custom-call | tf_op jit(solution)/shard_map/pallas_call | solution.py:374
  46.9 0.9 %copy.9 = f32[16,3,16,2,64]{4,3,2,1,0:T(2,128)} copy(f32[16,3,16,2,64]{4,3,2,1,0:T(2,128)S(1)} %bitcast.6) | data formatting | bytes 786432

commit v3 on v2

--- a/solution.py
+++ b/solution.py
@@ -60,34 +60,28 @@
         top = jnp.where(lane < snaps, top, swapped - whole[:snaps])
         grams.append(top)
         states.append(top + jnp.where(line == lane, ridge[pair], 0.0))
-    turned = [pltpu.roll(state, snaps, 1) * sign for state in states]
     for k in range(0, snaps, 2):
         near, far = line == k, line == k + 1
         column = (lane // 2 == k // 2) | (lane // 2 == (snaps + k) // 2)
         unit = jnp.where((near | far) & (lane == line), 1.0, 0.0)
-        other = jnp.where((near | far) & (lane == snaps + line), 1.0, 0.0)
         for pair in range(pairs):
-            state, twin = states[pair], turned[pair]
-            first_re, second_re = state[:, k:k + 1], state[:, k + 1:k + 2]
-            first_im, second_im = state[:, snaps + k:snaps + k + 1], state[:, snaps + k + 1:snaps + k + 2]
-            head, tail = state[k:k + 1, k:k + 1], state[k + 1:k + 2, k + 1:k + 2]
-            cross_re, cross_im = state[k:k + 1, k + 1:k + 2], state[k:k + 1, snaps + k + 1:snaps + k + 2]
+            state = states[pair]
+            first_re, second_re, first_im, second_im = (
+                jnp.broadcast_to(state[:, at:at + 1], state.shape) for at in (k, k + 1, snaps + k, snaps + k + 1))
+            head, tail = first_re[k:k + 1], second_re[k + 1:k + 2]
+            cross_re, cross_im = second_re[k:k + 1], second_im[k:k + 1]
             inverse = 1.0 / (head * tail - (cross_re * cross_re + cross_im * cross_im))
-            head, tail, cross_re, cross_im = head * inverse, tail * inverse, cross_re * inverse, cross_im * inverse
             cleared = jnp.where(column, unit, state)
-            cleared_twin = jnp.where(column, other, twin)
-            one, two = cleared[k:k + 1, :], cleared[k + 1:k + 2, :]
-            one_twin, two_twin = cleared_twin[k:k + 1, :], cleared_twin[k + 1:k + 2, :]
-            top = tail * one - (cross_re * two + cross_im * two_twin)
-            top_twin = tail * one_twin - (cross_re * two_twin - cross_im * two)
-            low = head * two - (cross_re * one - cross_im * one_twin)
-            low_twin = head * two_twin - (cross_re * one_twin + cross_im * one)
+            one, two = cleared[k:k + 1], cleared[k + 1:k + 2]
+            one_twin, two_twin = pltpu.roll(one, snaps, 1) * sign, pltpu.roll(two, snaps, 1) * sign
+            top = (tail * one - (cross_re * two + cross_im * two_twin)) * inverse
+            top_twin = (tail * one_twin - (cross_re * two_twin - cross_im * two)) * inverse
+            low = (head * two - (cross_re * one - cross_im * one_twin)) * inverse
+            low_twin = (head * two_twin - (cross_re * one_twin + cross_im * one)) * inverse
             fresh = cleared - ((first_re * top + first_im * top_twin) + (second_re * low + second_im * low_twin))
-            fresh_twin = cleared_twin - ((first_re * top_twin - first_im * top) + (second_re * low_twin - second_im * low))
             states[pair] = jnp.where(near, top, jnp.where(far, low, fresh))
-            turned[pair] = jnp.where(near, top_twin, jnp.where(far, low_twin, fresh_twin))
-    return [jnp.dot(grams[pair], jnp.concatenate([states[pair], turned[pair]], axis=0), precision=HIGHEST,
-                    preferred_element_type=jnp.float32) for pair in range(pairs)]
+    return [jnp.dot(grams[pair], jnp.concatenate([states[pair], pltpu.roll(states[pair], snaps, 1) * sign], axis=0),
+                    precision=HIGHEST, preferred_element_type=jnp.float32) for pair in range(pairs)]
 
 
 class Sizes:
@@ -276,6 +270,13 @@
                 rows = x_rows[pair, pl.ds((block // batch) * span, span), :]
                 term = lax.dot_general(rows, rows, (((0,), (0,)), ((), ())), precision=HIGHEST, preferred_element_type=jnp.float32)
                 gram[pair] = term if gram[pair] is None else gram[pair] + term
+    def collect(side):
+        which = half if side == 0 else 1 - half
+        for pair in range(z.pair_local):
+            for block in range(z.half_heights):
+                gather(y_in, lambda member: ((block * z.snap_count + member) * 2 + which) * z.out_stride, pair,
+                       y_rows.at[side, pair], block)
+
     small[2].wait()
     ridge = []
     for pair in range(z.pair_local):
@@ -287,20 +288,12 @@
         s_out[pair] = tops[pair]
     s_copy.start()
 
-    y_kept.wait()
-    each(y_copy, 1, z.half_owners, arrived)
     lane = lax.broadcasted_iota(jnp.int32, (1, LANES), 1)
-
-    def collect(side):
-        which = half if side == 0 else 1 - half
-        for pair in range(z.pair_local):
-            for block in range(z.half_heights):
-                gather(y_in, lambda member: ((block * z.snap_count + member) * 2 + which) * z.out_stride, pair,
-                       y_rows.at[side, pair], block)
 
     def fit(side, tops):
         misses = jnp.zeros((1, 1), jnp.float32)
         energy = jnp.zeros((1, 1), jnp.float32)
+        outcome = []
         for pair in range(z.pair_local):
             target = y_rows[side, pair]
             fitted = lax.dot_general(target, embed(tops[pair]), (((1,), (1,)), ((), ())), precision=HIGHEST,
@@ -308,29 +301,35 @@
             gap = target - fitted
             misses = misses + jnp.sum(gap * gap, keepdims=True)
             energy = energy + jnp.sum(target * target, keepdims=True)
+            outcome.append(fitted)
+        return outcome, jnp.where(lane == 0, misses, jnp.where(lane == 1, energy, 0.0))
+
+    def regroup(side, outcome, note):
+        for pair in range(z.pair_local):
             for block in range(z.half_heights):
                 for group in range(z.sets):
-                    moved = swap_groups([fitted[(block * z.groups + index) * TILE:(block * z.groups + index + 1) * TILE,
-                                                group * LANES:(group + 1) * LANES] for index in range(z.groups)], z.snap_local)
+                    moved = swap_groups([outcome[pair][(block * z.groups + index) * TILE:(block * z.groups + index + 1) * TILE,
+                                                       group * LANES:(group + 1) * LANES] for index in range(z.groups)], z.snap_local)
                     for index, piece in enumerate(moved):
                         row = place(lambda member: (block * z.snap_count + member) * z.back_stride, group * z.groups + index, pair)
                         b_out[side, pl.ds(row, z.tiles, stride=z.kinds), :] = piece[:z.tiles]
-        note = jnp.where(lane == 0, misses, jnp.where(lane == 1, energy, 0.0))
-        for step in range(z.half_owners):
-            b_out[side, pl.ds(step * z.back_stride + z.sent, 1), :] = note
-        return note
-
+        b_out[side, pl.ds(z.sent, z.half_owners, stride=z.back_stride), :] = jnp.broadcast_to(note, (z.half_owners, LANES))
+
+    y_kept.wait()
+    each(y_copy, 1, z.half_owners, arrived)
     collect(0)
-    note = fit(0, tops)
+    outcome, note = fit(0, tops)
+    regroup(0, outcome, note)
     b_kept[0].start()
     each(b_copy(0, own_slot), 1, z.half_owners, start)
     collect(1)
     s_copy.wait_recv()
-    note = note + fit(1, [s_in[pair] for pair in range(z.pair_local)])
+    outcome, twin_note = fit(1, [s_in[pair] for pair in range(z.pair_local)])
+    note_out[...] = jnp.broadcast_to(note + twin_note, note_out.shape)
+    each(note_copy, 0, z.half_owners, start)
+    regroup(1, outcome, twin_note)
     b_kept[1].start()
     each(b_copy(1, twin_slot), 1, z.half_owners, start)
-    note_out[...] = jnp.broadcast_to(note, note_out.shape)
-    each(note_copy, 0, z.half_owners, start)
 
     each(x_copy, 1, z.owners, sent)
     each(y_copy, 1, z.half_owners, sent)

time: 49.6 us -> 43.4 us (0.88)
  Pallas kernels: 46.2 us -> 40 us
    pallas_call x1, Pallas kernels: 46.2 us -> 40 us  [per_device(): pl.pallas_call(functools.partial(whole_kernel, z), in_specs=[hbm] * 5, ou...]
where the time goes in v3:
time: 43.4 us; the launch traced here: 43.2 us
  Pallas kernels  40 us (92%)
  between operations  2.33 us (5%)
  local copies, waits for them, and re-layouts  0.88 us (2%)
    pallas_call x1, Pallas kernels, per_device(): pl.pallas_call(functools.partial(whole_kernel, z), in_specs=[hbm] * 5, ou...  40 us
    unnamed x1, local copies, waits for them, and re-layouts  0.88 us

profile of v3, /device:TPU:0, one launch (start us, length us, event | category | flops | bytes accessed | tf_op | source)
XLA Modules:
  0.0 43.2 jit_solution(15330122474440311332)
XLA Ops:
  0.6 40.0 %shard_map.68 = (f32[1536,64]{1,0:T(8,128)S(1)}, f32[1,1]{1,0:T(1,128)}) custom-call(bf16[256,256]{1,0:T(8,128)(2,1)} %constant.2.clone.wave_hbm, s32[2,64]{1,0:T(2,128)} %bitcast.9, s32[1,64]{1,0:T(1,128)} %bitcast.10, bf16[16,48,32,128]{3,2,1,0:T(8,128)(2,1)} %bitcast.7, bf16[16,48,32,128]{3,2,1,0:T(8,128)(2,1)} %bitcast.8), custom_call_target="tpu_custom_call" | custom-call | tf_op jit(solution)/shard_map/pallas_call | solution.py:373
  40.7 0.9 %copy.9 = f32[16,3,16,2,64]{4,3,2,1,0:T(2,128)} copy(f32[16,3,16,2,64]{4,3,2,1,0:T(2,128)S(1)} %bitcast.6) | data formatting | bytes 786432

commit v4 on v3

--- a/solution.py
+++ b/solution.py
@@ -45,21 +45,20 @@
     return arrays
 
 
-def invert(gram, ridge):
-    pairs = len(gram)
-    snaps = gram[0].shape[0] // 2
+def fold(whole):
+    snaps = whole.shape[0] // 2
+    lane = lax.broadcasted_iota(jnp.int32, (snaps, 2 * snaps), 1)
+    swapped = pltpu.roll(whole[snaps:], snaps, 1)
+    return jnp.where(lane < snaps, whole[:snaps] + swapped, swapped - whole[:snaps])
+
+
+def invert(grams, ridge):
+    pairs = len(grams)
+    snaps = grams[0].shape[0]
     lane = lax.broadcasted_iota(jnp.int32, (snaps, 2 * snaps), 1)
     line = lax.broadcasted_iota(jnp.int32, (snaps, 2 * snaps), 0)
     sign = jnp.where(lax.broadcasted_iota(jnp.int32, (1, 2 * snaps), 1) < snaps, -1.0, 1.0)
-    grams = []
-    states = []
-    for pair in range(pairs):
-        whole = gram[pair]
-        swapped = pltpu.roll(whole[snaps:], snaps, 1)
-        top = whole[:snaps] + jnp.where(lane < snaps, swapped, 0.0)
-        top = jnp.where(lane < snaps, top, swapped - whole[:snaps])
-        grams.append(top)
-        states.append(top + jnp.where(line == lane, ridge[pair], 0.0))
+    states = [grams[pair] + jnp.where(line == lane, ridge[pair], 0.0) for pair in range(pairs)]
     for k in range(0, snaps, 2):
         near, far = line == k, line == k + 1
         column = (lane // 2 == k // 2) | (lane // 2 == (snaps + k) // 2)
@@ -114,10 +113,33 @@
     return jnp.concatenate([top, pltpu.roll(top, snaps, 1) * sign], axis=0)
 
 
+def pack(tops):
+    snaps = tops[0].shape[0]
+    lane = lax.broadcasted_iota(jnp.int32, (snaps, 2 * snaps), 1)
+    line = lax.broadcasted_iota(jnp.int32, (snaps, 2 * snaps), 0)
+    first = jnp.where(line >= lane, tops[0], pltpu.roll(tops[0], snaps, 1))
+    second = jnp.where(line >= lane - snaps, pltpu.roll(tops[1], snaps, 1), tops[1])
+    return jnp.where(lane < snaps, first, second)
+
+
+def unpack(packed):
+    snaps = packed.shape[0]
+    lane = lax.broadcasted_iota(jnp.int32, (snaps, snaps), 1)
+    line = lax.broadcasted_iota(jnp.int32, (snaps, snaps), 0)
+    turned = packed.T
+    tops = []
+    for pair in range(2):
+        plain, other = packed[:, pair * snaps:(pair + 1) * snaps], turned[pair * snaps:(pair + 1) * snaps]
+        real = jnp.where(line >= lane, plain, other)
+        imaginary = jnp.where(line < lane, plain, jnp.where(line > lane, -other, 0.0))
+        tops.append(jnp.concatenate([real, imaginary], axis=1))
+    return tops
+
+
 def whole_kernel(z, wave_hbm, list_hbm, ridge_hbm, x_hbm, y_hbm, predicted_ref, misfit_ref,
-                 wave, list_ref, ridge_ref, x_buf, y_buf, table, x_out, y_out, x_in, y_in, x_rows, y_rows, s_out, s_in,
+                 wave, list_ref, ridge_ref, x_buf, y_buf, table, x_out, y_out, x_in, y_in, x_rows, y_rows, g_out, g_in, s_out, s_in,
                  b_out, b_in, note_out, note_in,
-                 load_sem, x_send, x_recv, y_send, y_recv, s_send, s_recv, b_send, b_recv, note_send, note_recv, own_sem):
+                 load_sem, x_send, x_recv, y_send, y_recv, g_send, g_recv, s_send, s_recv, b_send, b_recv, note_send, note_recv, own_sem):
     snap, height = lax.axis_index("snap"), lax.axis_index("height")
     half, inner = height // z.half_heights, lax.rem(height, z.half_heights)
     own_slot = snap * z.height_count + inner * 2 + half
@@ -126,9 +148,6 @@
 
     def wrap(value, count):
         return lax.rem(value + count, count)
-
-    def slot_of(snap_at, height_at):
-        return snap_at * z.height_count + lax.rem(height_at, z.half_heights) * 2 + height_at // z.half_heights
 
     def away(step):
         return wrap(snap + lax.rem(step, z.snap_count), z.snap_count), wrap(height + step // z.snap_count, z.height_count)
@@ -205,10 +224,13 @@
     def arrived(item):
         item.wait_recv()
 
-    def x_copy(step):
-        where = away(step)
-        return remote(x_out.at[at(slot_of(*where), z.out_stride, z.sent)], x_in.at[at(step, z.out_stride, z.sent)],
-                      x_send.at[step], x_recv.at[step], where)
+    def x_copy(side):
+        def copy(step):
+            where = beside(step, 1, half)
+            slot = where[0] * z.height_count + lax.rem(where[1], z.half_heights) * 2 + (half if side == 0 else 1 - half)
+            return remote(x_out.at[at(slot, z.out_stride, z.sent)], x_in.at[side, at(step, z.out_stride, z.sent)],
+                          x_send.at[side, step], x_recv.at[side, step], where)
+        return copy
 
     def y_copy(step):
         where = beside(step, 1, half)
@@ -226,22 +248,24 @@
         return remote(note_out.at[pl.ds(0, 1)], note_in.at[at(step, TILE, 1)], note_send.at[step], note_recv.at[step],
                       beside(step, 1, 1 - half))
 
-    x_kept = pltpu.make_async_copy(x_out.at[at(own_slot, z.out_stride, z.sent)], x_in.at[at(0, z.out_stride, z.sent)], own_sem.at[0])
     y_kept = pltpu.make_async_copy(
         y_out.at[at(snap * z.height_count + inner * 2, z.out_stride, 2 * z.out_stride)],
         y_in.at[at(0, 2 * z.out_stride, 2 * z.out_stride)], own_sem.at[1])
     slots = (own_slot, twin_slot)
+    x_kept = [pltpu.make_async_copy(x_out.at[at(slots[side], z.out_stride, z.sent)], x_in.at[side, at(0, z.out_stride, z.sent)],
+                                    own_sem.at[4 * side]) for side in range(2)]
+    mirror = (snap, (1 - half) * z.half_heights + inner)
+    g_copy = remote(g_out, g_in, g_send, g_recv, mirror)
     b_kept = [pltpu.make_async_copy(b_out.at[side, at(0, z.back_stride, z.back)], b_in.at[at(slots[side], z.back_stride, z.back)],
                                     own_sem.at[2 + side]) for side in range(2)]
-    s_copy = remote(s_out, s_in, s_send, s_recv, (snap, (1 - half) * z.half_heights + inner))
+    s_copy = remote(s_out, s_in, s_send, s_recv, mirror)
 
     spectrum(x_buf, x_loads, x_out)
     pl.semaphore_wait(barrier, z.owners - 1)
-    x_kept.start()
-    each(x_copy, 1, z.owners, start)
+    for side in (1, 0):
+        x_kept[side].start()
+        each(x_copy(side), 1, z.half_owners, start)
     spectrum(y_buf, y_loads, y_out)
-    y_kept.start()
-    each(y_copy, 1, z.half_owners, start)
 
     def place(base, index, pair):
         part, member = index // z.snap_count, index % z.snap_count
@@ -254,22 +278,35 @@
             for index, piece in enumerate(moved):
                 target[pl.ds((block * z.groups + index) * TILE, z.tiles), group * LANES:(group + 1) * LANES] = piece
 
-    gram = [None] * z.pair_local
-    batch = min(4, z.height_count)
+    batch = min(4, z.half_heights)
     span = batch * z.groups * TILE
-    for block in range(z.height_count):
-        for member in range(z.snap_count):
-            step = block * z.snap_count + member
-            if step == 0:
-                x_kept.wait()
-            else:
-                x_copy(step).wait_recv()
-        for pair in range(z.pair_local):
-            gather(x_in, lambda member: (block * z.snap_count + member) * z.out_stride, pair, x_rows.at[pair], block)
-            if block % batch == batch - 1:
-                rows = x_rows[pair, pl.ds((block // batch) * span, span), :]
-                term = lax.dot_general(rows, rows, (((0,), (0,)), ((), ())), precision=HIGHEST, preferred_element_type=jnp.float32)
-                gram[pair] = term if gram[pair] is None else gram[pair] + term
+
+    def grams(side):
+        found = [None] * z.pair_local
+        for block in range(z.half_heights):
+            for member in range(z.snap_count):
+                step = block * z.snap_count + member
+                if step == 0:
+                    x_kept[side].wait()
+                else:
+                    x_copy(side)(step).wait_recv()
+            for pair in range(z.pair_local):
+                gather(x_in.at[side], lambda member: (block * z.snap_count + member) * z.out_stride, pair, x_rows.at[side, pair], block)
+                if block % batch == batch - 1:
+                    rows = x_rows[side, pair, pl.ds((block // batch) * span, span), :]
+                    term = lax.dot_general(rows, rows, (((0,), (0,)), ((), ())), precision=HIGHEST,
+                                           preferred_element_type=jnp.float32)
+                    found[pair] = term if found[pair] is None else found[pair] + term
+        return [pack([fold(found[index]), fold(found[index + 1])]) for index in range(0, z.pair_local, 2)]
+
+    for index, packed in enumerate(grams(1)):
+        g_out[index] = packed
+    g_copy.start()
+    y_kept.start()
+    each(y_copy, 1, z.half_owners, start)
+    own_grams = grams(0)
+    g_copy.wait_recv()
+    tops = [top for index, packed in enumerate(own_grams) for top in unpack(packed + g_in[index])]
     def collect(side):
         which = half if side == 0 else 1 - half
         for pair in range(z.pair_local):
@@ -283,9 +320,9 @@
         mine = lax.broadcasted_iota(jnp.int32, (1, z.pairs), 1) == pair * z.owners + own_slot
         level = jnp.sum(jnp.where(mine, ridge_ref[...], 0), axis=1, keepdims=True)
         ridge.append(lax.shift_left(jnp.ones_like(level), level).astype(jnp.float32) * (0.25 * z.snaps))
-    tops = invert(gram, ridge)
-    for pair in range(z.pair_local):
-        s_out[pair] = tops[pair]
+    tops = invert(tops, ridge)
+    for index in range(z.pair_local // 2):
+        s_out[index] = pack(tops[2 * index:2 * index + 2])
     s_copy.start()
 
     lane = lax.broadcasted_iota(jnp.int32, (1, LANES), 1)
@@ -324,14 +361,16 @@
     each(b_copy(0, own_slot), 1, z.half_owners, start)
     collect(1)
     s_copy.wait_recv()
-    outcome, twin_note = fit(1, [s_in[pair] for pair in range(z.pair_local)])
+    outcome, twin_note = fit(1, [top for index in range(z.pair_local // 2) for top in unpack(s_in[index])])
     note_out[...] = jnp.broadcast_to(note + twin_note, note_out.shape)
     each(note_copy, 0, z.half_owners, start)
     regroup(1, outcome, twin_note)
     b_kept[1].start()
     each(b_copy(1, twin_slot), 1, z.half_owners, start)
 
-    each(x_copy, 1, z.owners, sent)
+    for side in range(2):
+        each(x_copy(side), 1, z.half_owners, sent)
+    g_copy.wait_send()
     each(y_copy, 1, z.half_owners, sent)
     s_copy.wait_send()
     for side in range(2):
@@ -385,23 +424,26 @@
             pltpu.VMEM((z.columns, z.wide), jnp.bfloat16),
             pltpu.VMEM((out_rows, LANES), jnp.float32),
             pltpu.VMEM((out_rows, LANES), jnp.float32),
+            pltpu.VMEM((2, z.half_owners * z.out_stride, LANES), jnp.float32),
             pltpu.VMEM((out_rows, LANES), jnp.float32),
-            pltpu.VMEM((out_rows, LANES), jnp.float32),
-            pltpu.VMEM((z.pair_local, z.height_count * gathered, 2 * z.snaps), jnp.float32),
             pltpu.VMEM((2, z.pair_local, z.half_heights * gathered, 2 * z.snaps), jnp.float32),
-            pltpu.VMEM((z.pair_local, z.snaps, 2 * z.snaps), jnp.float32),
-            pltpu.VMEM((z.pair_local, z.snaps, 2 * z.snaps), jnp.float32),
+            pltpu.VMEM((2, z.pair_local, z.half_heights * gathered, 2 * z.snaps), jnp.float32),
+            pltpu.VMEM((z.pair_local // 2, z.snaps, 2 * z.snaps), jnp.float32),
+            pltpu.VMEM((z.pair_local // 2, z.snaps, 2 * z.snaps), jnp.float32),
+            pltpu.VMEM((z.pair_local // 2, z.snaps, 2 * z.snaps), jnp.float32),
+            pltpu.VMEM((z.pair_local // 2, z.snaps, 2 * z.snaps), jnp.float32),
             pltpu.VMEM((2, back_rows, LANES), jnp.float32),
             pltpu.VMEM((2 * back_rows, LANES), jnp.float32),
             pltpu.VMEM((TILE, LANES), jnp.float32),
             pltpu.VMEM((z.half_owners * TILE, LANES), jnp.float32),
             dma((2 * z.components + 3,)),
-            dma((z.owners,)), dma((z.owners,)),
+            dma((2, z.half_owners)), dma((2, z.half_owners)),
             dma((z.half_owners,)), dma((z.half_owners,)),
+            dma, dma,
             dma, dma,
             dma((2, z.half_owners)), dma((2, z.half_owners)),
             dma((z.half_owners,)), dma((z.half_owners,)),
-            dma((4,)),
+            dma((5,)),
         ],
         compiler_params=pltpu.CompilerParams(collective_id=0, has_side_effects=True, vmem_limit_bytes=VMEM_BYTES),
     )(stay(jnp.asarray(wave_table(z.points))), stay(pair_list.T), stay(ridge_index.reshape(1, z.pairs)),

time: 43.4 us -> 41.4 us (0.954)
  Pallas kernels: 40 us -> 38 us
    pallas_call x1, Pallas kernels: 40 us -> 38 us  [per_device(): pl.pallas_call(functools.partial(whole_kernel, z), in_specs=[hbm] * 5, ou...]
where the time goes in v4:
time: 41.4 us; the launch traced here: 41.2 us
  Pallas kernels  38 us (92%)
  between operations  2.33 us (6%)
  local copies, waits for them, and re-layouts  0.88 us (2%)
    pallas_call x1, Pallas kernels, per_device(): pl.pallas_call(functools.partial(whole_kernel, z), in_specs=[hbm] * 5, ou...  38 us
    unnamed x1, local copies, waits for them, and re-layouts  0.88 us

profile of v4, /device:TPU:0, one launch (start us, length us, event | category | flops | bytes accessed | tf_op | source)
XLA Modules:
  0.0 41.2 jit_solution(6918436371792053673)
XLA Ops:
  0.6 38.0 %shard_map.68 = (f32[1536,64]{1,0:T(8,128)S(1)}, f32[1,1]{1,0:T(1,128)}) custom-call(bf16[256,256]{1,0:T(8,128)(2,1)} %constant.2.clone.wave_hbm, s32[2,64]{1,0:T(2,128)} %bitcast.9, s32[1,64]{1,0:T(1,128)} %bitcast.10, bf16[16,48,32,128]{3,2,1,0:T(8,128)(2,1)} %bitcast.7, bf16[16,48,32,128]{3,2,1,0:T(8,128)(2,1)} %bitcast.8), custom_call_target="tpu_custom_call" | custom-call | tf_op jit(solution)/shard_map/pallas_call | solution.py:412
  38.7 0.9 %copy.9 = f32[16,3,16,2,64]{4,3,2,1,0:T(2,128)} copy(f32[16,3,16,2,64]{4,3,2,1,0:T(2,128)S(1)} %bitcast.6) | data formatting | bytes 786432

commit v5 on v4

--- a/solution.py
+++ b/solution.py
@@ -13,6 +13,7 @@
 LANES = 128
 TILE = 8
 VMEM_BYTES = 48 << 20
+UNROLLED = 16
 
 
 def wave_table(points):
@@ -107,6 +108,15 @@
         self.sets = 2 * snap_count // self.groups
 
 
+def three(left, right):
+    left_high, right_high = left.astype(jnp.bfloat16), right.astype(jnp.bfloat16)
+    left_low = (left - left_high.astype(jnp.float32)).astype(jnp.bfloat16)
+    right_low = (right - right_high.astype(jnp.float32)).astype(jnp.bfloat16)
+    return lax.dot_general(jnp.concatenate([left_high, left_high, left_low], axis=1),
+                           jnp.concatenate([right_high, right_low, right_high], axis=1),
+                           (((1,), (1,)), ((), ())), preferred_element_type=jnp.float32)
+
+
 def embed(top):
     snaps = top.shape[0]
     sign = jnp.where(lax.broadcasted_iota(jnp.int32, (1, 2 * snaps), 1) < snaps, -1.0, 1.0)
@@ -213,7 +223,11 @@
         def one(step, carry):
             act(copy(step))
             return carry
-        lax.fori_loop(first, last, one, 0)
+        if last > UNROLLED:
+            lax.fori_loop(first, last, one, 0)
+        else:
+            for step in range(first, last):
+                act(copy(step))
 
     def start(item):
         item.start()
@@ -333,8 +347,7 @@
         outcome = []
         for pair in range(z.pair_local):
             target = y_rows[side, pair]
-            fitted = lax.dot_general(target, embed(tops[pair]), (((1,), (1,)), ((), ())), precision=HIGHEST,
-                                     preferred_element_type=jnp.float32)
+            fitted = three(target, embed(tops[pair]))
             gap = target - fitted
             misses = misses + jnp.sum(gap * gap, keepdims=True)
             energy = energy + jnp.sum(target * target, keepdims=True)

time: 41.4 us -> 40.6 us (0.981)
  Pallas kernels: 38 us -> 37.2 us
    pallas_call x1, Pallas kernels: 38 us -> 37.2 us  [per_device(): pl.pallas_call(functools.partial(whole_kernel, z), in_specs=[hbm] * 5, ou...]
where the time goes in v5:
time: 40.6 us; the launch traced here: 40.4 us
  Pallas kernels  37.2 us (92%)
  between operations  2.33 us (6%)
  local copies, waits for them, and re-layouts  0.88 us (2%)
    pallas_call x1, Pallas kernels, per_device(): pl.pallas_call(functools.partial(whole_kernel, z), in_specs=[hbm] * 5, ou...  37.2 us
    unnamed x1, local copies, waits for them, and re-layouts  0.88 us

profile of v5, /device:TPU:0, one launch (start us, length us, event | category | flops | bytes accessed | tf_op | source)
XLA Modules:
  0.0 40.4 jit_solution(11685999281577228105)
XLA Ops:
  0.6 37.2 %shard_map.68 = (f32[1536,64]{1,0:T(8,128)S(1)}, f32[1,1]{1,0:T(1,128)}) custom-call(bf16[256,256]{1,0:T(8,128)(2,1)} %constant.2.clone.wave_hbm, s32[2,64]{1,0:T(2,128)} %bitcast.9, s32[1,64]{1,0:T(1,128)} %bitcast.10, bf16[16,48,32,128]{3,2,1,0:T(8,128)(2,1)} %bitcast.7, bf16[16,48,32,128]{3,2,1,0:T(8,128)(2,1)} %bitcast.8), custom_call_target="tpu_custom_call" | custom-call | tf_op jit(solution)/shard_map/pallas_call | solution.py:425
  37.9 0.9 %copy.9 = f32[16,3,16,2,64]{4,3,2,1,0:T(2,128)} copy(f32[16,3,16,2,64]{4,3,2,1,0:T(2,128)S(1)} %bitcast.6) | data formatting | bytes 786432

commit v6 on v5

--- a/solution.py
+++ b/solution.py
@@ -183,7 +183,11 @@
         pl.semaphore_signal(barrier, inc=1, device_id=away(step), device_id_type=pl.DeviceIdType.MESH)
         return carry
 
-    lax.fori_loop(1, z.owners, greet, 0)
+    if z.owners > 2 * UNROLLED:
+        lax.fori_loop(1, z.owners, greet, 0)
+    else:
+        for step in range(1, z.owners):
+            greet(step, 0)
 
     same = (lax.broadcasted_iota(jnp.int32, (z.pairs, z.pairs), 0)
             == lax.broadcasted_iota(jnp.int32, (z.pairs, z.pairs), 1))

time: 40.6 us -> 40.8 us (level)
  no operation moved by 1% of the time
where the time goes in v6:
time: 40.8 us; the launch traced here: 40.6 us
  Pallas kernels  37.4 us (92%)
  between operations  2.33 us (6%)
  local copies, waits for them, and re-layouts  0.88 us (2%)
    pallas_call x1, Pallas kernels, per_device(): pl.pallas_call(functools.partial(whole_kernel, z), in_specs=[hbm] * 5, ou...  37.4 us
    unnamed x1, local copies, waits for them, and re-layouts  0.88 us

profile of v6, /device:TPU:0, one launch (start us, length us, event | category | flops | bytes accessed | tf_op | source)
XLA Modules:
  0.0 40.6 jit_solution(5209273186145949491)
XLA Ops:
  0.6 37.4 %shard_map.68 = (f32[1536,64]{1,0:T(8,128)S(1)}, f32[1,1]{1,0:T(1,128)}) custom-call(bf16[256,256]{1,0:T(8,128)(2,1)} %constant.2.clone.wave_hbm, s32[2,64]{1,0:T(2,128)} %bitcast.9, s32[1,64]{1,0:T(1,128)} %bitcast.10, bf16[16,48,32,128]{3,2,1,0:T(8,128)(2,1)} %bitcast.7, bf16[16,48,32,128]{3,2,1,0:T(8,128)(2,1)} %bitcast.8), custom_call_target="tpu_custom_call" | custom-call | tf_op jit(solution)/shard_map/pallas_call | solution.py:429
  38.0 0.9 %copy.9 = f32[16,3,16,2,64]{4,3,2,1,0:T(2,128)} copy(f32[16,3,16,2,64]{4,3,2,1,0:T(2,128)S(1)} %bitcast.6) | data formatting | bytes 786432
